TPU v7x, 128 devices: a whole 4x4x4 slice. The times are simulated.
128 devices in a mesh: row: 16 (over y, x_lo, core), col: 8 (over x_hi, z).
Axes of the slice: x: 4 (x_hi: 2, x_lo: 2; x = x_hi * 2 + x_lo), y: 4, z: 4, core: 2. Of those that a mesh axis runs over, the one named last changes fastest.
Arguments:
- amplitudes: float32 [512, 32, 32, 32], P('col', 'row'), may hold values from -6 to 6
- integrals: float32 [1024, 16384], P('col', 'row'), may hold values from -0.1875 to 0.1875
- occ_energy: float32 [32], replicated, may hold values from -2 to -0.5
- vir_energy: float32 [512], replicated, may hold values from 0.3 to 3
Outputs:
- residual: float32 [16384, 16384], P('col', 'row')
All inputs are finite; a program needn't handle non-finite values.
Results may differ from a plain program's by a relative error of at most 0.00007.
Values sent between devices are 32-bit elements; how exact they have to be, the bound alone decides.
No kernel may reach another device: no remote copies, remote signals or barrier semaphores. Data moves between devices by JAX's collectives and lax.ppermute only.
A program may use at most 128 MiB of HBM per device.

v0:
```python
import jax
import jax.numpy as jnp
from jax import lax
from jax.sharding import PartitionSpec as P


def body(amplitudes, integrals, occ_energy, vir_energy):
    columns = integrals.shape[1]
    virtuals = amplitudes.shape[0]
    whole_w = lax.all_gather(integrals, "col", axis=0, tiled=True)
    occupied = amplitudes.shape[1] * lax.axis_size("row")
    portion = lax.all_gather(amplitudes, "row", axis=1, tiled=True)
    amount = portion.shape[1]
    flattened = portion.reshape(virtuals * amount, portion.shape[2] * portion.shape[3])
    product = jnp.dot(
        flattened, whole_w, preferred_element_type=jnp.float32, precision=lax.Precision.HIGHEST
    )
    folded = product.reshape(virtuals, amount, columns)
    summed = folded.reshape(virtuals * occupied, columns)
    height = summed.shape[0]
    gap_flat = (vir_energy[:, None] - occ_energy[None, :]).reshape(-1)
    row_gap = lax.dynamic_slice_in_dim(gap_flat, lax.axis_index("col") * height, height)
    col_gap = lax.dynamic_slice_in_dim(gap_flat, lax.axis_index("row") * columns, columns)
    return summed / (row_gap[:, None] + col_gap[None, :])


def solution(mesh):
    in_specs = (P("col", "row", None, None), P("col", "row"), P(), P())
    out_specs = P("col", "row")
    return jax.shard_map(body, mesh=mesh, in_specs=in_specs, out_specs=out_specs, check_vma=False)
```

profile of v0, /device:TPU:1, one launch (start us, length us, event | category | flops | bytes accessed | tf_op | source)
XLA Modules:
  0.0 217.1 jit_solution(794362143846984651)
XLA Ops:
  6.5 0.0 all-gather.3.cloned.1.call-start
  6.5 0.7 all-gather.3.cloned.1.call-update
  7.3 0.0 all-gather.5.cloned.1.call-start
  7.3 0.7 all-gather.5.cloned.1.call-update
  8.0 0.8 broadcast_subtract_fusion
  8.8 0.1 sub.20
  9.0 95.3 %all-gather.3.cloned.1.call-done = f32[64,32,32,32]{0,3,2,1:T(8,128)} async-done(((f32[64,2,32,32]{0,3,2,1:T(8,128)}), f32[64,32,32,32]{0,3,2,1:T(8,128)}) %all-gather.3.cloned.1.call-update) | async-done | bytes 8388624 | tf_op jit(solution)/shard_map/all_gather | solution.py:12
  104.3 30.4 %copy.6 = f32[64,32,32,32]{3,2,1,0:T(8,128)} copy(f32[64,32,32,32]{0,3,2,1:T(8,128)} %all-gather.3.cloned.1.call-done) | data formatting | bytes 16777216 | tf_op jit(solution)/shard_map/all_gather | solution.py:12
  134.7 26.3 %reshape.11 = f32[2048,1024]{1,0:T(8,128)} reshape(f32[64,32,32,32]{3,2,1,0:T(8,128)} %copy.6) | data formatting | bytes 16777216 | tf_op jit(solution)/shard_map/reshape | solution.py:14
  161.0 17.4 %all-gather.5.cloned.1.call-done = f32[1024,1024]{1,0:T(8,128)} async-done(((f32[128,1024]{1,0:T(8,128)}), f32[1024,1024]{1,0:T(8,128)}) %all-gather.5.cloned.1.call-update) | async-done | bytes 4194320 | tf_op jit(solution)/shard_map/all_gather | solution.py:10
  178.4 31.9 %add_divide_fusion = f32[2048,1024]{1,0:T(8,128)} fusion(f32[1024]{0:T(1024)S(1)} %dynamic_slice.7, f32[2048]{0:T(1024)S(1)} %dynamic_slice.6, f32[2048,1024]{1,0:T(8,128)} %reshape.11, f32[1024,1024]{1,0:T(8,128)} %all-gather.5.cloned.1.call-done), kind=kOutput, calls=%fused_computation | convolution fusion | flops 25773998080 | bytes 20983808 | tf_op jit(solution)/shard_map/dot_general | solution.py:15
  (2 shorter events, 0.0 us)
Async XLA Ops:
  6.5 97.8 %all-gather.3.cloned.1.call-start = ((), (), s32[]{:S(2)}) async-start(), calls=%async_computation | async-start | bytes 17825792 | tf_op jit(solution)/shard_map/all_gather | solution.py:12
  7.3 171.2 %all-gather.5.cloned.1.call-start = ((), (), s32[]{:S(2)}) async-start(), calls=%async_computation.1 | async-start | bytes 4718592 | tf_op jit(solution)/shard_map/all_gather | solution.py:10
Sparse Core Ops, SparseCore 0:
  9.1 95.2 all-gather.2
  106.7 71.7 all-gather.4
where the time goes:
time: 218 us; the launch traced here: 217 us
  waiting for transfers between devices  114 us (52%)
  local copies, waits for them, and re-layouts  56.8 us (26%)
  matrix products  31.9 us (15%)
  between operations  13.4 us (6%)
    all_gather x1, waiting for transfers between devices, body(): portion = lax.all_gather(amplitudes, 'row', axis=1, tiled=True)  95.3 us
    dot_general x1, matrix products, body(): jnp.dot(flattened, whole_w, preferred_element_type=jnp.float32, precision...  31.9 us
    all_gather x1, local copies, waits for them, and re-layouts, body(): portion = lax.all_gather(amplitudes, 'row', axis=1, tiled=True)  30.4 us
    reshape x1, local copies, waits for them, and re-layouts, body(): portion.reshape(virtuals * amount, portion.shape[2] * portion.shape[3])  26.3 us
    all_gather x1, waiting for transfers between devices, body(): whole_w = lax.all_gather(integrals, 'col', axis=0, tiled=True)  17.4 us
  transfers between devices with their start and end apart: 2, of which 2 were waited for; matrix products, arithmetic and copies ran while one was open for 27% of the time, Pallas kernels for 0%

commit v1 on v0

--- a/solution.py
+++ b/solution.py
@@ -9,7 +9,9 @@
     virtuals = amplitudes.shape[0]
     whole_w = lax.all_gather(integrals, "col", axis=0, tiled=True)
     occupied = amplitudes.shape[1] * lax.axis_size("row")
-    portion = lax.all_gather(amplitudes, "row", axis=1, tiled=True)
+    portion = jnp.concatenate(
+        lax.all_to_all(jnp.stack([amplitudes] * lax.axis_size("row")), "row", 0, 0), axis=1
+    )
     amount = portion.shape[1]
     flattened = portion.reshape(virtuals * amount, portion.shape[2] * portion.shape[3])
     product = jnp.dot(

time: 218 us -> 316 us (1.45)
  local copies, waits for them, and re-layouts: 56.8 us -> 114 us
  other arithmetic: 0.83 us -> 25.4 us
  waiting for transfers between devices: 114 us -> 122 us
  starting transfers between devices: 0.04 us -> 7.08 us
    all_to_all x0 -> x1, waiting for transfers between devices: none -> 122 us  [body(): lax.all_to_all(jnp.stack([amplitudes] * lax.axis_size('row')), 'row', 0, 0)]
    all_gather x1 -> x0, waiting for transfers between devices: 95.3 us -> none  [body(): portion = lax.all_gather(amplitudes, 'row', axis=1, tiled=True)]
    unnamed x0 -> x13, local copies, waits for them, and re-layouts: none -> 44.9 us
    all_gather x1 -> x0, local copies, waits for them, and re-layouts: 30.4 us -> none  [body(): portion = lax.all_gather(amplitudes, 'row', axis=1, tiled=True)]
    another operation x0 -> x1, local copies, waits for them, and re-layouts: none -> 26.1 us  [body(): portion.reshape(virtuals * amount, portion.shape[2] * portion.shape[3])]
    all_to_all x0 -> x1, other arithmetic: none -> 25.2 us  [body(): lax.all_to_all(jnp.stack([amplitudes] * lax.axis_size('row')), 'row', 0, 0)]
    all_gather x1, waiting for transfers between devices: 17.4 us -> 0.01 us  [body(): whole_w = lax.all_gather(integrals, 'col', axis=0, tiled=True)]
    reshape x1 -> x2, local copies, waits for them, and re-layouts: 26.3 us -> 41.9 us  [body(): jnp.concatenate(lax.all_to_all(jnp.stack([amplitudes] * lax.axis_size('ro...]
  transfers between devices with their start and end apart: 2 -> 2, of which waited for: 2 -> 1; matrix products, arithmetic and copies ran while one was open for 27% -> 35% of each run, Pallas kernels for 0% -> 0%
where the time goes in v1:
time: 316 us; the launch traced here: 314 us
  waiting for transfers between devices  122 us (39%)
  local copies, waits for them, and re-layouts  114 us (36%)
  matrix products  32.1 us (10%)
  other arithmetic  25.4 us (8%)
  between operations  13.5 us (4%)
  starting transfers between devices  7.08 us (2%)
    all_to_all x1, waiting for transfers between devices, body(): lax.all_to_all(jnp.stack([amplitudes] * lax.axis_size('row')), 'row', 0, 0)  122 us
    unnamed x13, local copies, waits for them, and re-layouts  44.9 us
    reshape x2, local copies, waits for them, and re-layouts, body(): jnp.concatenate(lax.all_to_all(jnp.stack([amplitudes] * lax.axis_size('ro...  41.9 us
    dot_general x1, matrix products, body(): jnp.dot(flattened, whole_w, preferred_element_type=jnp.float32, precision...  32.1 us
    another operation x1, local copies, waits for them, and re-layouts, body(): portion.reshape(virtuals * amount, portion.shape[2] * portion.shape[3])  26.1 us
    all_to_all x1, other arithmetic, body(): lax.all_to_all(jnp.stack([amplitudes] * lax.axis_size('row')), 'row', 0, 0)  25.2 us
    all_to_all x1, starting transfers between devices, body(): lax.all_to_all(jnp.stack([amplitudes] * lax.axis_size('row')), 'row', 0, 0)  7.05 us
  transfers between devices with their start and end apart: 2, of which 1 were waited for; matrix products, arithmetic and copies ran while one was open for 35% of the time, Pallas kernels for 0%

profile of v1, /device:TPU:1, one launch (start us, length us, event | category | flops | bytes accessed | tf_op | source)
XLA Modules:
  0.0 314.0 jit_solution(1659576743852906545)
XLA Ops:
  6.5 0.0 copy-start
  6.5 1.2 copy-done
  7.8 7.9 %broadcast_bitcast_fusion = f32[16,2,32,32,64]{4,3,2,1,0:T(8,128)} fusion(f32[64,2,32,32]{0,3,2,1:T(8,128)S(1)} %copy-done), kind=kLoop, calls=%fused_computation.3 | loop fusion | bytes 8912896
  15.7 18.4 %reshape.14 = f32[16,1,131072]{2,1,0:T(1,128)} reshape(f32[16,2,32,32,64]{4,3,2,1,0:T(8,128)} %broadcast_bitcast_fusion) | data formatting | bytes 16777216
  34.1 0.0 copy-start.3
  34.1 0.0 copy-start.4
  34.1 7.0 %all-to-all-start = ((f32[16,1,131072]{2,1,0:T(1,128)}), f32[16,1,131072]{2,1,0:T(1,128)}, u32[]{:S(2)}, u32[]{:S(2)}) async-start(f32[16,1,131072]{2,1,0:T(1,128)} %reshape.14), calls=%async_computation | async-start | bytes 16777216 | tf_op jit(solution)/shard_map/all_to_all | solution.py:13
  41.1 0.0 all-gather.2.cloned.1.call-start
  41.2 0.7 all-gather.2.cloned.1.call-update
  41.9 0.0 copy-done.3
  41.9 0.0 copy-done.4
  41.9 0.1 broadcast_subtract_fusion
  42.0 0.1 sub.20
  42.1 0.0 copy-start.2
  42.2 121.7 %all-to-all-done = f32[16,1,131072]{2,1,0:T(1,128)} async-done(((f32[16,1,131072]{2,1,0:T(1,128)}), f32[16,1,131072]{2,1,0:T(1,128)}, u32[]{:S(2)}, u32[]{:S(2)}) %all-to-all-start) | async-done | bytes 8388640 | tf_op jit(solution)/shard_map/all_to_all | solution.py:13
  163.8 0.5 broadcast.8
  164.3 25.2 %reduce = f32[16,131072]{1,0:T(8,128)} reduce(f32[16,1,131072]{2,1,0:T(1,128)} %all-to-all-done, f32[]{:T(128)} %broadcast.8), dimensions={1}, to_apply=%all_to_all.3.reduce_sub_computation | reduce | bytes 16777220 | tf_op jit(solution)/shard_map/all_to_all | solution.py:13
  189.6 0.0 copy-done.2
  189.6 17.4 %reshape.15 = f32[16,2,32,32,64]{4,3,2,1,0:T(8,128)} reshape(f32[16,131072]{1,0:T(8,128)} %reduce) | data formatting | bytes 16777216
  206.9 11.6 %bitcast_bitcast_fusion = f32[64,16,2,32,32]{0,4,3,2,1:T(8,128)} fusion(f32[16,2,32,32,64]{4,3,2,1,0:T(8,128)} %reshape.15), kind=kLoop, calls=%fused_computation.2 | loop fusion | bytes 16777216 | tf_op jit(solution)/shard_map/reshape | solution.py:12
  218.5 30.4 %copy.7 = f32[64,16,2,32,32]{4,3,2,1,0:T(8,128)} copy(f32[64,16,2,32,32]{0,4,3,2,1:T(8,128)} %bitcast_bitcast_fusion) | data formatting | bytes 16777216 | tf_op jit(solution)/shard_map/reshape | solution.py:12
  248.9 0.0 dynamic-slice-start
  248.9 0.0 dynamic-slice-start.1
  248.9 26.1 %reshape_reshape.3 = f32[2048,1024]{1,0:T(8,128)} reshape(f32[64,16,2,32,32]{4,3,2,1,0:T(8,128)} %copy.7) | data formatting | bytes 16777216 | tf_op jit(solution)/shard_map/reshape;reshape | solution.py:16
  274.9 0.0 all-gather.2.cloned.1.call-done
  274.9 0.0 dynamic-slice-done
  274.9 0.0 dynamic-slice-done.1
  275.0 0.0 copy-start.1
  275.0 32.1 %add_divide_fusion = f32[2048,1024]{1,0:T(8,128)} fusion(f32[1024]{0:T(1024)S(1)} %dynamic-slice-done.1, f32[2048]{0:T(1024)S(1)} %dynamic-slice-done, f32[2048,1024]{1,0:T(8,128)} %reshape_reshape.3, f32[1024,1024]{1,0:T(8,128)} %all-gather.2.cloned.1.call-done), kind=kOutput, calls=%fused_computation | convolution fusion | flops 25773998080 | bytes 20983808 | tf_op jit(solution)/shard_map/dot_general | solution.py:17
  307.1 0.0 copy-done.1
Async XLA Ops:
  6.5 1.2 copy-start
  34.1 7.8 %copy-start.3 = (f32[512]{0:T(512)S(1)}, f32[512]{0:T(512)}, u32[]{:S(2)}) copy-start(f32[512]{0:T(512)} %param.7) | copy-start | bytes 6148
  34.1 7.8 %copy-start.4 = (f32[32]{0:T(128)S(1)}, f32[32]{0:T(128)}, u32[]{:S(2)}) copy-start(f32[32]{0:T(128)} %param.6) | copy-start | bytes 388
  34.1 129.7 %all-to-all-start = ((f32[16,1,131072]{2,1,0:T(1,128)}), f32[16,1,131072]{2,1,0:T(1,128)}, u32[]{:S(2)}, u32[]{:S(2)}) async-start(f32[16,1,131072]{2,1,0:T(1,128)} %reshape.14), calls=%async_computation | async-start | bytes 16777216 | tf_op jit(solution)/shard_map/all_to_all | solution.py:13
  41.1 233.8 %all-gather.2.cloned.1.call-start = ((), (), s32[]{:S(2)}) async-start(), calls=%async_computation.1 | async-start | bytes 4718592 | tf_op jit(solution)/shard_map/all_gather | solution.py:10
  42.1 147.4 %copy-start.2 = (f32[16384]{0:T(1024)}, f32[16384]{0:T(1024)S(1)}, u32[]{:S(2)}) copy-start(f32[16384]{0:T(1024)S(1)} %sub.20) | copy-start | bytes 196612
  248.9 26.1 %dynamic-slice-start = ((f32[16384]{0:T(1024)}, s32[]{:T(128)}), f32[2048]{0:T(1024)S(1)}, s32[]{:S(2)}) async-start(f32[16384]{0:T(1024)} %copy-done.2, s32[]{:T(128)} %select_n.6), calls=%async_computation.2 | async-start | bytes 16896 | tf_op jit(solution)/shard_map/dynamic_slice | solution.py:24
  248.9 26.1 %dynamic-slice-start.1 = ((f32[16384]{0:T(1024)}, s32[]{:T(128)}), f32[1024]{0:T(1024)S(1)}, s32[]{:S(2)}) async-start(f32[16384]{0:T(1024)} %copy-done.2, s32[]{:T(128)} %select_n.7), calls=%async_computation.3 | async-start | bytes 8704 | tf_op jit(solution)/shard_map/dynamic_slice | solution.py:25
  275.0 32.2 %copy-start.1 = (f32[64,2,32,32]{0,3,2,1:T(8,128)S(1)}, f32[64,2,32,32]{0,3,2,1:T(8,128)}, u32[]{:S(2)}) copy-start(f32[64,2,32,32]{0,3,2,1:T(8,128)} %param.4) | copy-start | bytes 1572868
Sparse Core Ops, SparseCore 0:
  44.3 101.6 all-gather.1
